TPU v7x, 32 devices: a whole 2x2x4 slice. The times are simulated.
32 devices in a mesh: seq: 16 (over z, y, x), head: 2 (over core).
Axes of the slice: x: 2, y: 2, z: 4, core: 2. Of those that a mesh axis runs over, the one named last changes fastest.
Arguments:
- latents: bfloat16 [2048, 1536], P('seq'), may hold values from -6 to 6
- caption: bfloat16 [512, 4096], P('seq'), may hold values from -6 to 6
- conditioning: bfloat16 [2, 1024], replicated, may hold values from -6 to 6
- clip_frames: int32 [2], replicated, may hold values from 4 to 16, as said below
- valid_patches: int32 [2], replicated, may hold values from 192 to 384, as said below
- query_proj: bfloat16 [1536, 1536], P('seq', 'head'), may hold values from -0.15625 to 0.15625
- key_proj: bfloat16 [1536, 1536], P('seq', 'head'), may hold values from -0.15625 to 0.15625
- value_proj: bfloat16 [1536, 1536], P('seq', 'head'), may hold values from -0.15625 to 0.15625
- output_proj: bfloat16 [1536, 1536], P('head', 'seq'), may hold values from -1.5 to 1.5
- caption_key: bfloat16 [4096, 1536], P('seq', 'head'), may hold values from -0.09375 to 0.09375
- caption_value: bfloat16 [4096, 1536], P('seq', 'head'), may hold values from -0.09375 to 0.09375
- gate_proj: bfloat16 [1536, 4096], P('seq', 'head'), may hold values from -0.15625 to 0.15625
- up_proj: bfloat16 [1536, 4096], P('seq', 'head'), may hold values from -0.15625 to 0.15625
- down_proj: bfloat16 [4096, 1536], P('head', 'seq'), may hold values from -0.09375 to 0.09375
- modulation: bfloat16 [1024, 6144], P('seq'), may hold values from -0.1875 to 0.1875
- query_gain: float32 [64], replicated, may hold values from 0.5 to 1.5
- key_gain: float32 [64], replicated, may hold values from 0.5 to 1.5
- caption_gain: float32 [64], replicated, may hold values from 0.5 to 1.5
- attn_gain: float32 [1536], replicated, may hold values from 0.5 to 1.5
- ffn_gain: float32 [1536], replicated, may hold values from 0.5 to 1.5
- cross_gate: float32 [24], P('head'), may hold values from 0.3 to 1.5
- cotangent: bfloat16 [2048, 1536], P('seq'), may hold values from -6 to 6
Outputs:
- output: bfloat16 [2048, 1536], P('seq')
- grad_latents: bfloat16 [2048, 1536], P('seq')
- grad_query_proj: float32 [1536, 1536], P('seq', 'head')
- grad_key_proj: float32 [1536, 1536], P('seq', 'head')
- grad_value_proj: float32 [1536, 1536], P('seq', 'head')
- grad_output_proj: float32 [1536, 1536], P('head', 'seq')
- grad_caption_key: float32 [4096, 1536], P('seq', 'head')
- grad_caption_value: float32 [4096, 1536], P('seq', 'head')
- grad_gate_proj: float32 [1536, 4096], P('seq', 'head')
- grad_up_proj: float32 [1536, 4096], P('seq', 'head')
- grad_down_proj: float32 [4096, 1536], P('head', 'seq')
- grad_modulation: float32 [1024, 6144], P('seq')
- grad_query_gain: float32 [64], replicated
- grad_key_gain: float32 [64], replicated
- grad_caption_gain: float32 [64], replicated
- grad_attn_gain: float32 [1536], replicated
- grad_ffn_gain: float32 [1536], replicated
- grad_cross_gate: float32 [24], P('head')
Inputs may be any that keep to these rules, and one draw needn't show every extreme that they name: `clip_frames`: the clips lie end to end from the first token; their frames together cover more than all 2048 tokens, and the tokens of the last clips that lie past the end do not exist. One of the first two clips has 16 frames and the other 4. In every frame of a clip the first valid_patches of its 384 patch tokens are in use, the rest are padding; the frame's last token is the nextframe token. One of the first two clips uses all 384 and the other 192.
All inputs are finite; a program needn't handle non-finite values.
Results may differ from a plain program's by a relative error of at most 0.02.
Values may be sent and summed in bfloat16 or wider, within the bound.
No kernel may reach another device: no remote copies, remote signals or barrier semaphores. Data moves between devices by JAX's collectives and lax.ppermute only.
A program may use at most 256 MiB of HBM per device.

v0:
```python
import math

import jax
import jax.numpy as jnp
from jax import lax
from jax.sharding import PartitionSpec as P

TEXT = 256
FRAME = 385


EPSILON = 1e-06
HIGHEST = lax.Precision.HIGHEST


def token_layout(clip_frames, valid_patches, first, count):
    clips = clip_frames.shape[0]
    ends = FRAME * jnp.cumsum(clip_frames)
    starts = ends - FRAME * clip_frames
    places = first + jnp.arange(count, dtype=jnp.int32)
    clip_index = jnp.sum((ends[None, :] <= places[:, None]).astype(jnp.int32), axis=1)
    chosen = (clip_index[:, None] == jnp.arange(clips, dtype=jnp.int32)[None, :]).astype(jnp.int32)
    position = places - jnp.sum(chosen * starts[None, :], axis=1)
    within = position % FRAME
    limit = jnp.sum(chosen * valid_patches[None, :], axis=1)
    valid = (within < limit) | (within == FRAME - 1)
    tag = jnp.where(valid, clip_index, -1)
    return (clip_index, position, tag)


def rotate(values, position, sign):
    half = values.shape[-1] // 2
    rates = 10000.0 ** (-(jnp.arange(half, dtype=jnp.float32) * 2.0 / values.shape[-1]))
    angle = position.astype(jnp.float32)[:, None] * rates[None, :]
    cosine = jnp.cos(angle)[:, None, :]
    sine = sign * jnp.sin(angle)[:, None, :]
    first = values[..., :half]
    second = values[..., half:]
    return jnp.concatenate(
        [first * cosine - second * sine, first * sine + second * cosine], axis=-1
    )


def head_norm(values, gain):
    return values * lax.rsqrt(jnp.mean(values * values, axis=-1, keepdims=True) + EPSILON) * gain


def norm_back(raw, gain, grad):
    inverse = lax.rsqrt(jnp.mean(raw * raw, axis=-1, keepdims=True) + EPSILON)
    unit = raw * inverse
    scaled = grad * gain
    back = inverse * (scaled - unit * jnp.mean(scaled * unit, axis=-1, keepdims=True))
    return (back, grad * unit)


def contract_rows(left, right):
    return lax.dot_general(
        left, right, (((0,), (0,)), ((), ())), preferred_element_type=jnp.float32
    )


def contract_cols(left, right):
    return lax.dot_general(
        left, right, (((1,), (1,)), ((), ())), preferred_element_type=jnp.float32
    )


def split_parts(values):
    upper = values.astype(jnp.bfloat16)
    lower = (values - upper.astype(jnp.float32)).astype(jnp.bfloat16)
    return (upper, lower)


def block_rows(count):
    for option in (512, 256, 128, 64, 32, 16, 8):
        return option
    return count


def over_blocks(step, state, arrays):
    count = arrays[0].shape[0]
    width = block_rows(count)
    stacked = tuple((array.reshape((count // width, width) + array.shape[1:]) for array in arrays))

    def inner(carry, parts):
        return (step(carry, parts), None)

    result, unused = lax.scan(inner, state, stacked)
    return result


def body(
    latents,
    caption,
    conditioning,
    clip_frames,
    valid_patches,
    query_proj,
    key_proj,
    value_proj,
    output_proj,
    caption_key,
    caption_value,
    gate_proj,
    up_proj,
    down_proj,
    modulation,
    query_gain,
    key_gain,
    caption_gain,
    attn_gain,
    ffn_gain,
    cross_gate,
    cotangent,
):
    rows_here = latents.shape[0]
    width = latents.shape[1]
    head_dim = query_gain.shape[0]
    heads_here = cross_gate.shape[0]
    inner_width = heads_here * head_dim
    clips = conditioning.shape[0]
    scale = 1.0 / math.sqrt(head_dim)
    seq_place = lax.axis_index("seq")
    clip_index, position, tag = token_layout(
        clip_frames, valid_patches, seq_place * rows_here, rows_here
    )
    clip_float = clip_index.astype(jnp.float32)
    key_tag = tag.astype(jnp.float32)
    tag_send = tag.astype(jnp.bfloat16)
    clip_send = clip_index.astype(jnp.bfloat16)
    onehot = (clip_index[:, None] == jnp.arange(clips, dtype=jnp.int32)[None, :]).astype(
        jnp.float32
    )
    gathered = (
        lax.all_gather(query_proj, "seq", axis=0, tiled=True),
        lax.all_gather(key_proj, "seq", axis=0, tiled=True),
        lax.all_gather(value_proj, "seq", axis=0, tiled=True),
        lax.all_gather(output_proj, "seq", axis=1, tiled=True),
        lax.all_gather(caption_key, "seq", axis=0, tiled=True),
        lax.all_gather(caption_value, "seq", axis=0, tiled=True),
        lax.all_gather(gate_proj, "seq", axis=0, tiled=True),
        lax.all_gather(up_proj, "seq", axis=0, tiled=True),
        lax.all_gather(down_proj, "seq", axis=1, tiled=True),
        lax.all_gather(modulation, "seq", axis=0, tiled=True),
    )
    (
        query_all,
        key_all,
        value_all,
        output_all,
        caption_key_all,
        caption_value_all,
        gate_all,
        up_all,
        down_all,
        modulation_all,
    ) = gathered
    silu_cond = jax.nn.silu(conditioning.astype(jnp.float32)).astype(jnp.bfloat16)
    shifts = jnp.dot(silu_cond, modulation_all, preferred_element_type=jnp.float32)
    per_token = jnp.dot(onehot, shifts, precision=HIGHEST)
    scale_attn = per_token[:, :width]
    gate_attn = per_token[:, width : 2 * width]
    scale_ffn = per_token[:, 2 * width : 3 * width]
    gate_ffn = per_token[:, 3 * width :]
    inputs = latents.astype(jnp.float32)
    first_mult = attn_gain * (1.0 + scale_attn)
    first_unit = inputs * lax.rsqrt(jnp.mean(inputs * inputs, axis=-1, keepdims=True) + EPSILON)
    normed = (first_unit * first_mult).astype(jnp.bfloat16)
    query_raw = jnp.dot(normed, query_all, preferred_element_type=jnp.float32).reshape(
        rows_here, heads_here, head_dim
    )
    key_raw = jnp.dot(normed, key_all, preferred_element_type=jnp.float32).reshape(
        rows_here, heads_here, head_dim
    )
    values = jnp.dot(normed, value_all, preferred_element_type=jnp.float32).astype(jnp.bfloat16)
    queries = rotate(head_norm(query_raw, query_gain), position, 1.0).astype(jnp.bfloat16)
    keys = (
        rotate(head_norm(key_raw, key_gain), position, 1.0)
        .astype(jnp.bfloat16)
        .reshape(rows_here, inner_width)
    )
    keys_heads = keys.reshape(rows_here, heads_here, head_dim)
    values_heads = values.reshape(rows_here, heads_here, head_dim)
    own_text = caption.shape[0]
    caption_raw = jnp.dot(caption, caption_key_all, preferred_element_type=jnp.float32).reshape(
        own_text, heads_here, head_dim
    )
    caption_keys_own = (
        head_norm(caption_raw, caption_gain).astype(jnp.bfloat16).reshape(own_text, inner_width)
    )
    caption_values_own = jnp.dot(
        caption, caption_value_all, preferred_element_type=jnp.float32
    ).astype(jnp.bfloat16)
    caption_keys, caption_values = (
        lax.all_gather(caption_keys_own, "seq", axis=0, tiled=True),
        lax.all_gather(caption_values_own, "seq", axis=0, tiled=True),
    )
    text_rows = caption_keys.shape[0]
    text_clip = (jnp.arange(text_rows, dtype=jnp.int32) // TEXT).astype(jnp.float32)
    caption_keys_heads = caption_keys.reshape(text_rows, heads_here, head_dim)
    caption_values_heads = caption_values.reshape(text_rows, heads_here, head_dim)
    start_state = (
        jnp.zeros((heads_here, rows_here), jnp.float32),
        jnp.zeros((rows_here, heads_here, head_dim), jnp.float32),
    )
    piece = (
        lax.all_gather(keys, "seq", axis=0, tiled=True),
        lax.all_gather(values, "seq", axis=0, tiled=True),
        lax.all_gather(tag_send, "seq", axis=0, tiled=True),
    )

    def step(inner_state, parts):
        total, weighted = inner_state
        key_block, value_block, tag_block = parts
        count = key_block.shape[0]
        key_heads = key_block.reshape(count, heads_here, head_dim)
        value_heads = value_block.reshape(count, heads_here, head_dim)
        scores = (
            jnp.einsum("qhd,khd->hqk", queries, key_heads, preferred_element_type=jnp.float32)
            * scale
        )
        allowed = (clip_float[:, None] == tag_block.astype(jnp.float32)[None, :])[None]
        weights = jnp.where(allowed, jnp.exp(scores), 0.0)
        total = total + jnp.sum(weights, axis=-1)
        weighted = weighted + jnp.einsum(
            "hqk,khd->qhd",
            weights.astype(jnp.bfloat16),
            value_heads,
            preferred_element_type=jnp.float32,
        )
        return (total, weighted)

    self_total, self_weighted = over_blocks(step, start_state, piece)
    self_out = self_weighted / self_total.T[:, :, None]
    cross_allowed = (clip_float[:, None] == text_clip[None, :])[None]
    cross_scores = (
        jnp.einsum("qhd,khd->hqk", queries, caption_keys_heads, preferred_element_type=jnp.float32)
        * scale
    )
    cross_weights = jnp.where(cross_allowed, jnp.exp(cross_scores), 0.0)
    cross_total = jnp.sum(cross_weights, axis=-1)
    cross_low = cross_weights.astype(jnp.bfloat16)
    cross_out = (
        jnp.einsum(
            "hqk,khd->qhd", cross_low, caption_values_heads, preferred_element_type=jnp.float32
        )
        / cross_total.T[:, :, None]
    )
    gates = jnp.tanh(cross_gate)[None, :, None]
    mixed = (self_out + gates * cross_out).astype(jnp.bfloat16).reshape(rows_here, inner_width)
    attended = lax.psum(
        jnp.dot(mixed, output_all, preferred_element_type=jnp.float32).astype(jnp.bfloat16), "head"
    ).astype(jnp.float32)
    attn_tanh = jnp.tanh(gate_attn)
    hidden = inputs + attn_tanh * attended
    second_mult = ffn_gain * (1.0 + scale_ffn)
    second_unit = hidden * lax.rsqrt(jnp.mean(hidden * hidden, axis=-1, keepdims=True) + EPSILON)
    ffn_input = (second_unit * second_mult).astype(jnp.bfloat16)
    gate_val = jnp.dot(ffn_input, gate_all, preferred_element_type=jnp.float32)
    up_val = jnp.dot(ffn_input, up_all, preferred_element_type=jnp.float32)
    sigma = jax.nn.sigmoid(gate_val)
    activation = (gate_val * sigma * up_val).astype(jnp.bfloat16)
    ffn_out = lax.psum(
        jnp.dot(activation, down_all, preferred_element_type=jnp.float32).astype(jnp.bfloat16),
        "head",
    ).astype(jnp.float32)
    ffn_tanh = jnp.tanh(gate_ffn)
    output = (hidden + ffn_tanh * ffn_out).astype(jnp.bfloat16)
    regathered = (
        lax.all_gather(query_proj, "seq", axis=0, tiled=True),
        lax.all_gather(key_proj, "seq", axis=0, tiled=True),
        lax.all_gather(value_proj, "seq", axis=0, tiled=True),
        lax.all_gather(output_proj, "seq", axis=1, tiled=True),
        lax.all_gather(gate_proj, "seq", axis=0, tiled=True),
        lax.all_gather(up_proj, "seq", axis=0, tiled=True),
        lax.all_gather(down_proj, "seq", axis=1, tiled=True),
    )
    query_back, key_back, value_back, output_back, gate_back, up_back, down_back = regathered
    upstream = cotangent.astype(jnp.float32)
    d_ffn = (ffn_tanh * upstream).astype(jnp.bfloat16)
    grad_down = contract_rows(activation, d_ffn)
    d_act = contract_cols(d_ffn, down_back)
    d_gate = (d_act * up_val * sigma * (1.0 + gate_val * (1.0 - sigma))).astype(jnp.bfloat16)
    d_up = (d_act * gate_val * sigma).astype(jnp.bfloat16)
    grad_gate = contract_rows(ffn_input, d_gate)
    grad_up = contract_rows(ffn_input, d_up)
    d_ffn_input = lax.psum(contract_cols(d_gate, gate_back) + contract_cols(d_up, up_back), "head")
    second_back, second_terms = norm_back(hidden, second_mult, d_ffn_input)
    ffn_gain_part = jnp.sum(second_terms * (1.0 + scale_ffn), axis=0)
    d_scale_ffn = second_terms * ffn_gain
    d_gate_ffn = upstream * ffn_out * (1.0 - ffn_tanh * ffn_tanh)
    d_hidden = upstream + second_back
    d_attended = (attn_tanh * d_hidden).astype(jnp.bfloat16)
    d_gate_attn = d_hidden * attended * (1.0 - attn_tanh * attn_tanh)
    grad_output = contract_rows(mixed, d_attended)
    d_mixed = (
        contract_cols(d_attended, output_back)
        .astype(jnp.bfloat16)
        .reshape(rows_here, heads_here, head_dim)
    )
    d_mixed_float = d_mixed.astype(jnp.float32)
    cross_tanh = jnp.tanh(cross_gate)
    cross_gate_part = jnp.sum(d_mixed_float * cross_out, axis=(0, 2)) * (
        1.0 - cross_tanh * cross_tanh
    )
    d_cross = (gates * d_mixed_float).astype(jnp.bfloat16)
    d_cross_float = d_cross.astype(jnp.float32)
    cross_prob = cross_weights / cross_total[:, :, None]
    cross_dprob = jnp.einsum(
        "qhd,khd->hqk", d_cross, caption_values_heads, preferred_element_type=jnp.float32
    )
    cross_delta = jnp.sum(d_cross_float * cross_out, axis=-1).T
    cross_ds = (cross_prob * (cross_dprob - cross_delta[:, :, None])).astype(jnp.bfloat16)
    dquery_cross = (
        jnp.einsum("hqk,khd->qhd", cross_ds, caption_keys_heads, preferred_element_type=jnp.float32)
        * scale
    )
    caption_dkey = (
        jnp.einsum("hqk,qhd->khd", cross_ds, queries, preferred_element_type=jnp.float32) * scale
    )
    cross_upper, cross_lower = split_parts(d_cross_float / cross_total.T[:, :, None])
    caption_dvalue = jnp.einsum(
        "hqk,qhd->khd", cross_low, cross_upper, preferred_element_type=jnp.float32
    ) + jnp.einsum("hqk,qhd->khd", cross_low, cross_lower, preferred_element_type=jnp.float32)
    caption_terms = jnp.concatenate(
        [
            caption_dkey.reshape(text_rows, inner_width),
            caption_dvalue.reshape(text_rows, inner_width),
        ],
        axis=1,
    )
    inverse_total = 1.0 / self_total.T
    self_delta = jnp.sum(d_mixed_float * self_out, axis=-1)
    piece = (
        lax.all_gather(keys, "seq", axis=0, tiled=True),
        lax.all_gather(values, "seq", axis=0, tiled=True),
        lax.all_gather(tag_send, "seq", axis=0, tiled=True),
    )

    def step(inner_state, parts):
        key_block, value_block, tag_block = parts
        count = key_block.shape[0]
        key_heads = key_block.reshape(count, heads_here, head_dim)
        value_heads = value_block.reshape(count, heads_here, head_dim)
        scores = (
            jnp.einsum("qhd,khd->hqk", queries, key_heads, preferred_element_type=jnp.float32)
            * scale
        )
        allowed = (clip_float[:, None] == tag_block.astype(jnp.float32)[None, :])[None]
        prob = jnp.where(allowed, jnp.exp(scores), 0.0) * inverse_total.T[:, :, None]
        prob_grad = jnp.einsum(
            "qhd,khd->hqk", d_mixed, value_heads, preferred_element_type=jnp.float32
        )
        score_grad = (prob * (prob_grad - self_delta.T[:, :, None])).astype(jnp.bfloat16)
        return (
            inner_state
            + jnp.einsum("hqk,khd->qhd", score_grad, key_heads, preferred_element_type=jnp.float32)
            * scale
        )

    dquery_self = over_blocks(
        step, jnp.zeros((rows_here, heads_here, head_dim), jnp.float32), piece
    )
    stats_inverse, stats_delta = (
        lax.all_gather(inverse_total, "seq", axis=0, tiled=True),
        lax.all_gather(self_delta, "seq", axis=0, tiled=True),
    )
    key_start = (
        jnp.zeros((rows_here, heads_here, head_dim), jnp.float32),
        jnp.zeros((rows_here, heads_here, head_dim), jnp.float32),
    )
    query_rows = lax.all_gather(queries.reshape(rows_here, inner_width), "seq", axis=0, tiled=True)
    grad_rows = lax.all_gather(d_mixed.reshape(rows_here, inner_width), "seq", axis=0, tiled=True)
    clip_rows = lax.all_gather(clip_send, "seq", axis=0, tiled=True)
    count = query_rows.shape[0]

    def step(inner_state, parts):
        query_block, grad_block, clip_block, inverse_block, delta_block = parts
        block_count = query_block.shape[0]
        query_heads = query_block.reshape(block_count, heads_here, head_dim)
        grad_heads = grad_block.reshape(block_count, heads_here, head_dim)
        scores = (
            jnp.einsum("qhd,khd->hqk", query_heads, keys_heads, preferred_element_type=jnp.float32)
            * scale
        )
        allowed = (clip_block.astype(jnp.float32)[:, None] == key_tag[None, :])[None]
        weights = jnp.where(allowed, jnp.exp(scores), 0.0)
        prob = weights * inverse_block.T[:, :, None]
        prob_grad = jnp.einsum(
            "qhd,khd->hqk", grad_heads, values_heads, preferred_element_type=jnp.float32
        )
        score_grad = (prob * (prob_grad - delta_block.T[:, :, None])).astype(jnp.bfloat16)
        key_grad, value_grad = inner_state
        key_grad = (
            key_grad
            + jnp.einsum(
                "hqk,qhd->khd", score_grad, query_heads, preferred_element_type=jnp.float32
            )
            * scale
        )
        weights_low = weights.astype(jnp.bfloat16)
        grad_upper, grad_lower = split_parts(
            grad_heads.astype(jnp.float32) * inverse_block[:, :, None]
        )
        value_grad = (
            value_grad
            + jnp.einsum(
                "hqk,qhd->khd", weights_low, grad_upper, preferred_element_type=jnp.float32
            )
            + jnp.einsum(
                "hqk,qhd->khd", weights_low, grad_lower, preferred_element_type=jnp.float32
            )
        )
        return (key_grad, value_grad)

    dkey_self, dvalue_self = over_blocks(
        step, key_start, (query_rows, grad_rows, clip_rows, stats_inverse, stats_delta)
    )
    caption_sums = lax.psum_scatter(caption_terms, "seq", scatter_dimension=0, tiled=True)
    dkey_caption = caption_sums[:, :inner_width].reshape(own_text, heads_here, head_dim)
    dvalue_caption = caption_sums[:, inner_width:].astype(jnp.bfloat16)
    dcaption_raw, caption_terms_gain = norm_back(caption_raw, caption_gain, dkey_caption)
    grad_caption_key = contract_rows(
        caption, dcaption_raw.astype(jnp.bfloat16).reshape(own_text, inner_width)
    )
    grad_caption_value = contract_rows(caption, dvalue_caption)
    dquery_turned = rotate(dquery_self + dquery_cross, position, -1.0)
    dquery_raw, query_terms = norm_back(query_raw, query_gain, dquery_turned)
    dkey_turned = rotate(dkey_self, position, -1.0)
    dkey_raw, key_terms = norm_back(key_raw, key_gain, dkey_turned)
    dquery_low = dquery_raw.astype(jnp.bfloat16).reshape(rows_here, inner_width)
    dkey_low = dkey_raw.astype(jnp.bfloat16).reshape(rows_here, inner_width)
    dvalue_low = dvalue_self.astype(jnp.bfloat16).reshape(rows_here, inner_width)
    grad_query = contract_rows(normed, dquery_low)
    grad_key = contract_rows(normed, dkey_low)
    grad_value = contract_rows(normed, dvalue_low)
    normed_part = (
        contract_cols(dquery_low, query_back)
        + contract_cols(dkey_low, key_back)
        + contract_cols(dvalue_low, value_back)
    )
    gain_parts = jnp.stack(
        [
            jnp.sum(query_terms, axis=(0, 1)),
            jnp.sum(key_terms, axis=(0, 1)),
            jnp.sum(caption_terms_gain, axis=(0, 1)),
        ]
    )
    d_normed, gain_heads = (
        lax.psum(normed_part.astype(jnp.bfloat16), "head").astype(jnp.float32),
        lax.psum(gain_parts.astype(jnp.bfloat16), "head").astype(jnp.float32),
    )
    first_back, first_terms = norm_back(inputs, first_mult, d_normed)
    grad_latents = (d_hidden + first_back).astype(jnp.bfloat16)
    attn_gain_part = jnp.sum(first_terms * (1.0 + scale_attn), axis=0)
    d_scale_attn = first_terms * attn_gain
    token_grads = jnp.concatenate([d_scale_attn, d_gate_attn, d_scale_ffn, d_gate_ffn], axis=1)
    shift_part = lax.dot_general(onehot, token_grads, (((0,), (0,)), ((), ())), precision=HIGHEST)
    shift_grad, grad_attn_gain, grad_ffn_gain, grad_cross_gate, gain_grads = lax.psum(
        (shift_part, attn_gain_part, ffn_gain_part, cross_gate_part, gain_heads), "seq"
    )
    cond_rows = modulation.shape[0]
    silu_local = lax.dynamic_slice_in_dim(silu_cond, seq_place * cond_rows, cond_rows, 1).astype(
        jnp.float32
    )
    grad_modulation = lax.dot_general(
        silu_local, shift_grad, (((0,), (0,)), ((), ())), precision=HIGHEST
    )
    shards = (
        lax.psum_scatter(grad_query, "seq", scatter_dimension=0, tiled=True),
        lax.psum_scatter(grad_key, "seq", scatter_dimension=0, tiled=True),
        lax.psum_scatter(grad_value, "seq", scatter_dimension=0, tiled=True),
        lax.psum_scatter(grad_output, "seq", scatter_dimension=1, tiled=True),
        lax.psum_scatter(grad_caption_key, "seq", scatter_dimension=0, tiled=True),
        lax.psum_scatter(grad_caption_value, "seq", scatter_dimension=0, tiled=True),
        lax.psum_scatter(grad_gate, "seq", scatter_dimension=0, tiled=True),
        lax.psum_scatter(grad_up, "seq", scatter_dimension=0, tiled=True),
        lax.psum_scatter(grad_down, "seq", scatter_dimension=1, tiled=True),
    )
    (
        shard_query,
        shard_key,
        shard_value,
        shard_output,
        shard_caption_key,
        shard_caption_value,
        shard_gate,
        shard_up,
        shard_down,
    ) = shards
    return (
        output,
        grad_latents,
        shard_query,
        shard_key,
        shard_value,
        shard_output,
        shard_caption_key,
        shard_caption_value,
        shard_gate,
        shard_up,
        shard_down,
        grad_modulation,
        gain_grads[0],
        gain_grads[1],
        gain_grads[2],
        grad_attn_gain,
        grad_ffn_gain,
        grad_cross_gate,
    )


def solution(mesh):
    placed = (
        P("seq", None),
        P("seq", None),
        P(),
        P(),
        P(),
        P("seq", "head"),
        P("seq", "head"),
        P("seq", "head"),
        P("head", "seq"),
        P("seq", "head"),
        P("seq", "head"),
        P("seq", "head"),
        P("seq", "head"),
        P("head", "seq"),
        P("seq", None),
        P(),
        P(),
        P(),
        P(),
        P(),
        P("head"),
        P("seq", None),
    )
    return jax.shard_map(
        body,
        mesh=mesh,
        in_specs=placed,
        out_specs=(
            P("seq", None),
            P("seq", None),
            P("seq", "head"),
            P("seq", "head"),
            P("seq", "head"),
            P("head", "seq"),
            P("seq", "head"),
            P("seq", "head"),
            P("seq", "head"),
            P("seq", "head"),
            P("head", "seq"),
            P("seq", None),
            P(),
            P(),
            P(),
            P(),
            P(),
            P("head"),
        ),
        check_vma=False,
    )
```

profile of v0, /device:TPU:0, one launch (start us, length us, event | category | flops | bytes accessed | tf_op | source)
XLA Modules:
  0.0 3057.9 jit_solution(13462030379562757002)
XLA Ops:
  16.0 149.6 %all-gather.17.cloned.1.call-done = bf16[1024,6144]{1,0:T(8,128)(2,1)} async-done(((bf16[64,6144]{1,0:T(8,128)(2,1)}), bf16[1024,6144]{1,0:T(8,128)(2,1)}) %all-gather.17.cloned.1.call-update) | async-done | bytes 12582928 | tf_op jit(solution)/shard_map/all_gather | solution.py:144
  175.3 53.6 %all-gather.23.cloned.1.call-done = bf16[1536,768]{1,0:T(8,128)(2,1)} async-done(((bf16[96,768]{1,0:T(8,128)(2,1)}), bf16[1536,768]{1,0:T(8,128)(2,1)}) %all-gather.23.cloned.1.call-update) | async-done | bytes 2359312 | tf_op jit(solution)/shard_map/all_gather | solution.py:135
  231.2 61.6 %all-gather.19.cloned.1.call-done = bf16[1536,768]{1,0:T(8,128)(2,1)} async-done(((bf16[96,768]{1,0:T(8,128)(2,1)}), bf16[1536,768]{1,0:T(8,128)(2,1)}) %all-gather.19.cloned.1.call-update) | async-done | bytes 2359312 | tf_op jit(solution)/shard_map/all_gather | solution.py:136
  296.6 60.0 %all-gather.25.cloned.1.call-done = bf16[1536,768]{1,0:T(8,128)(2,1)} async-done(((bf16[96,768]{1,0:T(8,128)(2,1)}), bf16[1536,768]{1,0:T(8,128)(2,1)}) %all-gather.25.cloned.1.call-update) | async-done | bytes 2359312 | tf_op jit(solution)/shard_map/all_gather | solution.py:137
  360.4 38.5 %all-gather = bf16[16,1,128]{2,1,0:T(2,128)(2,1)S(1)} all-gather(bf16[1,1,128]{2,1,0:T(2,128)(2,1)S(1)} %convert_bitcast_fusion.4), channel_id=1, replica_groups=mesh['seq'=16,'head'=2] {'seq'}, dimensions={0}, use_global_device_ids=true | all-gather | bytes 4352 | tf_op jit(solution)/shard_map/all_gather | solution.py:209
  399.1 53.4 %all-gather.31.cloned.1.call-done = bf16[4096,768]{1,0:T(8,128)(2,1)} async-done(((bf16[256,768]{1,0:T(8,128)(2,1)}), bf16[4096,768]{1,0:T(8,128)(2,1)}) %all-gather.31.cloned.1.call-update) | async-done | bytes 6291472 | tf_op jit(solution)/shard_map/all_gather | solution.py:139
  458.2 46.9 %all_gather.80 = bf16[512,768]{1,0:T(8,128)(2,1)S(1)} all-gather(bf16[32,768]{1,0:T(8,128)(2,1)S(1)} %get-tuple-element.540), channel_id=1, replica_groups=mesh['seq'=16,'head'=2] {'seq'}, dimensions={0}, use_global_device_ids=true | all-gather | bytes 835584 | tf_op jit(solution)/shard_map/all_gather | solution.py:195
  505.3 48.2 %all-gather.29.cloned.1.call-done = bf16[4096,768]{1,0:T(8,128)(2,1)} async-done(((bf16[256,768]{1,0:T(8,128)(2,1)}), bf16[4096,768]{1,0:T(8,128)(2,1)}) %all-gather.29.cloned.1.call-update) | async-done | bytes 6291472 | tf_op jit(solution)/shard_map/all_gather | solution.py:140
  557.4 46.2 %all_gather.78 = bf16[512,768]{1,0:T(8,128)(2,1)S(1)} all-gather(bf16[32,768]{1,0:T(8,128)(2,1)S(1)} %convolution_convert_fusion.4), channel_id=1, replica_groups=mesh['seq'=16,'head'=2] {'seq'}, dimensions={0}, use_global_device_ids=true | all-gather | bytes 835584 | tf_op jit(solution)/shard_map/all_gather | solution.py:196
  631.4 65.3 %all-gather.27.cloned.1.call-done = bf16[2048,768]{1,0:T(8,128)(2,1)} async-done(((bf16[128,768]{1,0:T(8,128)(2,1)}), bf16[2048,768]{1,0:T(8,128)(2,1)}) %all-gather.27.cloned.1.call-update) | async-done | bytes 3145744 | tf_op jit(solution)/shard_map/all_gather | solution.py:208
  784.4 95.3 %all-gather.35.cloned.1.call-done = bf16[1536,2048]{1,0:T(8,128)(2,1)} async-done(((bf16[96,2048]{1,0:T(8,128)(2,1)}), bf16[1536,2048]{1,0:T(8,128)(2,1)}) %all-gather.35.cloned.1.call-update) | async-done | bytes 6291472 | tf_op jit(solution)/shard_map/all_gather | solution.py:141
  884.7 90.6 %all-gather.37.cloned.1.call-done = bf16[1536,2048]{1,0:T(8,128)(2,1)} async-done(((bf16[96,2048]{1,0:T(8,128)(2,1)}), bf16[1536,2048]{1,0:T(8,128)(2,1)}) %all-gather.37.cloned.1.call-update) | async-done | bytes 6291472 | tf_op jit(solution)/shard_map/all_gather | solution.py:142
  980.1 90.7 %all-gather.39.cloned.1.call-done = bf16[2048,1536]{0,1:T(8,128)(2,1)} async-done(((bf16[2048,96]{0,1:T(8,128)(2,1)}), bf16[2048,1536]{0,1:T(8,128)(2,1)}) %all-gather.39.cloned.1.call-update) | async-done | bytes 6291472 | tf_op jit(solution)/shard_map/all_gather | solution.py:143
  1279.4 72.9 %while.39 = (s32[]{:T(128)}, f32[128,12,64]{0,2,1:T(8,128)}, f32[128,12,64]{0,2,1:T(8,128)}, bf16[4,512,768]{2,1,0:T(8,128)(2,1)}, bf16[4,512]{1,0:T(4,128)(2,1)...) while((s32[]{:T(128)}, f32[128,12,64]{0,2,1:T(8,128)}, ...), condition=%wide.region_23.24_spmd.clone, body=%wide.region_22.23_spmd.clone.sunk | while | flops 516948480 | bytes 29267632 | solution.py:88
  1469.5 79.3 %all-reduce = (f32[2,6144]{1,0:T(2,128)S(1)}, f32[3,64]{1,0:T(4,128)S(1)}, f32[1536]{0:T(1024)}, f32[1536]{0:T(1024)}, f32[12]{0:T(128)}) all-reduce(f32[2,6144]{1,0:T(2,128)S(1)} %fusion.42, bf16[3,64]{1,0:T(4,128)(2,1)S(1)} %psum.75, f32[1536]{0:T(1024)S(1)} %get-tuple-element.559, ...), channel_id=1, replica_groups=mesh['seq'=16,'head'=2] {'seq'}, use_global_device_ids=true, to_apply=%region_38.39 | all-reduce | flops 15564 | bytes 124128 | tf_op jit(solution)/shard_map/psum | solution.py:459
  1553.9 87.3 %reduce-scatter.21.cloned.1.call-done = f32[256,768]{0,1:T(8,128)} async-done(((f32[4096,768]{0,1:T(8,128)}), f32[256,768]{0,1:T(8,128)}) %reduce-scatter.21.cloned.1.call-update) | async-done | bytes 786448 | tf_op jit(solution)/shard_map/reduce_scatter | solution.py:474
  1643.5 206.9 %reduce-scatter.23.cloned.1.call-done = f32[256,768]{0,1:T(8,128)} async-done(((f32[4096,768]{0,1:T(8,128)}), f32[256,768]{0,1:T(8,128)}) %reduce-scatter.23.cloned.1.call-update) | async-done | bytes 786448 | tf_op jit(solution)/shard_map/reduce_scatter | solution.py:475
  1852.6 140.8 %reduce-scatter.17.cloned.1.call-done = f32[768,96]{0,1:T(8,128)} async-done(((f32[768,1536]{0,1:T(8,128)}), f32[768,96]{0,1:T(8,128)}) %reduce-scatter.17.cloned.1.call-update) | async-done | bytes 294928 | tf_op jit(solution)/shard_map/reduce_scatter | solution.py:473
  1993.4 142.2 %reduce-scatter.13.cloned.1.call-done = f32[96,768]{1,0:T(8,128)} async-done(((f32[1536,768]{1,0:T(8,128)}), f32[96,768]{1,0:T(8,128)}) %reduce-scatter.13.cloned.1.call-update) | async-done | bytes 294928 | tf_op jit(solution)/shard_map/reduce_scatter | solution.py:471
  2135.6 142.6 %reduce-scatter.11.cloned.1.call-done = f32[96,768]{1,0:T(8,128)} async-done(((f32[1536,768]{1,0:T(8,128)}), f32[96,768]{1,0:T(8,128)}) %reduce-scatter.11.cloned.1.call-update) | async-done | bytes 294928 | tf_op jit(solution)/shard_map/reduce_scatter | solution.py:470
  2278.2 141.9 %reduce-scatter.15.cloned.1.call-done = f32[96,768]{1,0:T(8,128)} async-done(((f32[1536,768]{1,0:T(8,128)}), f32[96,768]{1,0:T(8,128)}) %reduce-scatter.15.cloned.1.call-update) | async-done | bytes 294928 | tf_op jit(solution)/shard_map/reduce_scatter | solution.py:472
  2420.1 210.2 %reduce-scatter.25.cloned.1.call-done = f32[96,2048]{1,0:T(8,128)} async-done(((f32[1536,2048]{1,0:T(8,128)}), f32[96,2048]{1,0:T(8,128)}) %reduce-scatter.25.cloned.1.call-update) | async-done | bytes 786448 | tf_op jit(solution)/shard_map/reduce_scatter | solution.py:476
  2630.2 209.7 %reduce-scatter.27.cloned.1.call-done = f32[96,2048]{1,0:T(8,128)} async-done(((f32[1536,2048]{1,0:T(8,128)}), f32[96,2048]{1,0:T(8,128)}) %reduce-scatter.27.cloned.1.call-update) | async-done | bytes 786448 | tf_op jit(solution)/shard_map/reduce_scatter | solution.py:477
  2840.0 210.6 %reduce-scatter.29.cloned.1.call-done = f32[2048,96]{0,1:T(8,128)} async-done(((f32[2048,1536]{0,1:T(8,128)}), f32[2048,96]{0,1:T(8,128)}) %reduce-scatter.29.cloned.1.call-update) | async-done | bytes 786448 | tf_op jit(solution)/shard_map/reduce_scatter | solution.py:478
  (528 shorter events, 626.5 us)
Async XLA Ops:
  7.9 220.9 %all-gather.23.cloned.1.call-start = ((), (), s32[]{:S(2)}) async-start(), calls=%async_computation.13 | async-start | bytes 2506752 | tf_op jit(solution)/shard_map/all_gather | solution.py:135
  8.7 284.1 %all-gather.19.cloned.1.call-start = ((), (), s32[]{:S(2)}) async-start(), calls=%async_computation.11 | async-start | bytes 2506752 | tf_op jit(solution)/shard_map/all_gather | solution.py:136
  9.4 347.2 %all-gather.25.cloned.1.call-start = ((), (), s32[]{:S(2)}) async-start(), calls=%async_computation.14 | async-start | bytes 2506752 | tf_op jit(solution)/shard_map/all_gather | solution.py:137
  10.0 442.4 %all-gather.31.cloned.1.call-start = ((), (), s32[]{:S(2)}) async-start(), calls=%async_computation.17 | async-start | bytes 6684672 | tf_op jit(solution)/shard_map/all_gather | solution.py:139
  10.6 543.0 %all-gather.29.cloned.1.call-start = ((), (), s32[]{:S(2)}) async-start(), calls=%async_computation.16 | async-start | bytes 6684672 | tf_op jit(solution)/shard_map/all_gather | solution.py:140
  11.2 615.5 %all-gather.21.cloned.1.call-start = ((), (), s32[]{:S(2)}) async-start(), calls=%async_computation.12 | async-start | bytes 3342336 | tf_op jit(solution)/shard_map/all_gather | solution.py:207
  296.6 400.2 %all-gather.27.cloned.1.call-start = ((), (), s32[]{:S(2)}) async-start(), calls=%async_computation.15 | async-start | bytes 3342336 | tf_op jit(solution)/shard_map/all_gather | solution.py:208
  359.5 400.9 %all-gather.33.cloned.1.call-start = ((), (), s32[]{:S(2)}) async-start(), calls=%async_computation.18 | async-start | bytes 2506752 | tf_op jit(solution)/shard_map/all_gather | solution.py:138
  360.2 421.1 %all-reduce.6.cloned.1.call-start = ((), (), s32[]{:S(2)}) async-start(), calls=%async_computation.19 | async-start | bytes 786432 | tf_op jit(solution)/shard_map/psum | solution.py:251
  764.6 210.7 %all-gather.37.cloned.1.call-start = ((), (), s32[]{:S(2)}) async-start(), calls=%async_computation.21 | async-start | bytes 6684672 | tf_op jit(solution)/shard_map/all_gather | solution.py:142
  765.1 305.7 %all-gather.39.cloned.1.call-start = ((), (), s32[]{:S(2)}) async-start(), calls=%async_computation.22 | async-start | bytes 6684672 | tf_op jit(solution)/shard_map/all_gather | solution.py:143
  765.9 412.5 %all-reduce.8.cloned.1.call-start = ((), (), s32[]{:S(2)}) async-start(), calls=%async_computation.23 | async-start | bytes 1572864 | tf_op jit(solution)/shard_map/psum | solution.py:287
  1085.2 193.8 %all-gather.41.cloned.1.call-start = ((), (), s32[]{:S(2)}) async-start(), calls=%async_computation.24 | async-start | bytes 3342336 | tf_op jit(solution)/shard_map/all_gather | solution.py:372
  1087.0 192.0 %all-gather.43.cloned.1.call-start = ((), (), s32[]{:S(2)}) async-start(), calls=%async_computation.25 | async-start | bytes 3342336 | tf_op jit(solution)/shard_map/all_gather | solution.py:373
  1196.5 209.1 %reduce-scatter.19.cloned.1.call-start = ((), (), s32[]{:S(2)}) async-start(), calls=%async_computation.30 | async-start | bytes 3342336 | tf_op jit(solution)/shard_map/reduce_scatter | solution.py:419
  1369.8 271.4 %reduce-scatter.21.cloned.1.call-start = ((), (), s32[]{:S(2)}) async-start(), calls=%async_computation.31 | async-start | bytes 13369344 | tf_op jit(solution)/shard_map/reduce_scatter | solution.py:474
  1414.5 435.9 %reduce-scatter.23.cloned.1.call-start = ((), (), s32[]{:S(2)}) async-start(), calls=%async_computation.32 | async-start | bytes 13369344 | tf_op jit(solution)/shard_map/reduce_scatter | solution.py:475
  1421.8 571.6 %reduce-scatter.17.cloned.1.call-start = ((), (), s32[]{:S(2)}) async-start(), calls=%async_computation.29 | async-start | bytes 5013504 | tf_op jit(solution)/shard_map/reduce_scatter | solution.py:473
  1425.9 709.7 %reduce-scatter.13.cloned.1.call-start = ((), (), s32[]{:S(2)}) async-start(), calls=%async_computation.27 | async-start | bytes 5013504 | tf_op jit(solution)/shard_map/reduce_scatter | solution.py:471
  1429.9 848.3 %reduce-scatter.11.cloned.1.call-start = ((), (), s32[]{:S(2)}) async-start(), calls=%async_computation.26 | async-start | bytes 5013504 | tf_op jit(solution)/shard_map/reduce_scatter | solution.py:470
  1433.0 987.1 %reduce-scatter.15.cloned.1.call-start = ((), (), s32[]{:S(2)}) async-start(), calls=%async_computation.28 | async-start | bytes 5013504 | tf_op jit(solution)/shard_map/reduce_scatter | solution.py:472
  1437.0 1193.2 %reduce-scatter.25.cloned.1.call-start = ((), (), s32[]{:S(2)}) async-start(), calls=%async_computation.33 | async-start | bytes 13369344 | tf_op jit(solution)/shard_map/reduce_scatter | solution.py:476
  1444.7 1395.3 %reduce-scatter.27.cloned.1.call-start = ((), (), s32[]{:S(2)}) async-start(), calls=%async_computation.34 | async-start | bytes 13369344 | tf_op jit(solution)/shard_map/reduce_scatter | solution.py:477
  1452.1 1598.5 %reduce-scatter.29.cloned.1.call-start = ((), (), s32[]{:S(2)}) async-start(), calls=%async_computation.35 | async-start | bytes 13369344 | tf_op jit(solution)/shard_map/reduce_scatter | solution.py:478
  (115 other events, 6245.2 us)
Sparse Core Ops, SparseCore 0:
  10.8 154.7 all-gather.16
  168.4 60.4 all-gather.22
  231.7 61.0 all-gather.18
  295.5 61.0 all-gather.24
  359.2 93.1 all-gather.30
  455.1 98.4 all-gather.28
  556.9 69.7 all-gather.20
  630.1 66.6 all-gather.26
  699.5 60.7 all-gather.32
  784.4 95.3 all-gather.34
  882.8 92.4 all-gather.36
  978.4 92.4 all-gather.38
  1105.5 69.4 all-gather.40
  1196.6 66.0 all-gather.42
  1278.8 126.6 reduce-scatter.18
  1433.5 207.6 reduce-scatter.20
  1646.7 203.6 reduce-scatter.22
  1856.9 136.4 reduce-scatter.16
  1999.1 136.4 reduce-scatter.12
  2142.2 135.9 reduce-scatter.10
  2283.8 136.2 reduce-scatter.14
  2427.2 202.9 reduce-scatter.24
  2636.3 203.6 reduce-scatter.26
  2847.0 203.5 reduce-scatter.28
  (3 shorter events, 53.1 us)
where the time goes:
time: 3070 us; the launch traced here: 3060 us
  waiting for transfers between devices  2370 us (77%)
  blocking collectives  326 us (11%)
  matrix products  199 us (6%)
  local copies, waits for them, and re-layouts  110 us (4%)
  other arithmetic  37.5 us (1%)
    reduce_scatter x1, waiting for transfers between devices, body(): lax.psum_scatter(grad_down, 'seq', scatter_dimension=1, tiled=True)  211 us
    reduce_scatter x1, waiting for transfers between devices, body(): lax.psum_scatter(grad_gate, 'seq', scatter_dimension=0, tiled=True)  210 us
    reduce_scatter x1, waiting for transfers between devices, body(): lax.psum_scatter(grad_up, 'seq', scatter_dimension=0, tiled=True)  210 us
    reduce_scatter x1, waiting for transfers between devices, body(): lax.psum_scatter(grad_caption_value, 'seq', scatter_dimension=0, tiled=True)  207 us
    all_gather x1, waiting for transfers between devices, body(): lax.all_gather(modulation, 'seq', axis=0, tiled=True)  150 us
    reduce_scatter x1, waiting for transfers between devices, body(): lax.psum_scatter(grad_query, 'seq', scatter_dimension=0, tiled=True)  143 us
    reduce_scatter x1, waiting for transfers between devices, body(): lax.psum_scatter(grad_key, 'seq', scatter_dimension=0, tiled=True)  142 us
    reduce_scatter x1, waiting for transfers between devices, body(): lax.psum_scatter(grad_value, 'seq', scatter_dimension=0, tiled=True)  142 us
  transfers between devices with their start and end apart: 27, of which 23 were waited for; matrix products, arithmetic and copies ran while one was open for 10% of the time, Pallas kernels for 0%

commit v1 on v0

v1 whole, which is shorter than its diff:
```python
import math

import jax
import jax.numpy as jnp
from jax import lax
from jax.sharding import PartitionSpec as P

TEXT = 256
FRAME = 385
GROUPS = 4
EPSILON = 1e-06
LOW = jnp.bfloat16
FULL = jnp.float32


def token_layout(clip_frames, valid_patches, ids):
    clips = clip_frames.shape[0]
    upto = jnp.arange(clips)[None, :] <= jnp.arange(clips)[:, None]
    ends = FRAME * jnp.sum(jnp.where(upto, clip_frames[None, :], 0), axis=1)
    starts = ends - FRAME * clip_frames
    clip = jnp.sum((ends[None, :] <= ids[:, None]).astype(jnp.int32), axis=1)
    chosen = (clip[:, None] == jnp.arange(clips, dtype=jnp.int32)[None, :]).astype(jnp.int32)
    position = ids - jnp.sum(chosen * starts[None, :], axis=1)
    within = position % FRAME
    limit = jnp.sum(chosen * valid_patches[None, :], axis=1)
    tag = jnp.where((within < limit) | (within == FRAME - 1), clip, -1)
    return clip, position, tag


def rotate(values, cosine, sine):
    half = values.shape[-1] // 2
    first, second = values[..., :half], values[..., half:]
    return jnp.concatenate([first * cosine - second * sine, first * sine + second * cosine], -1)


def inverse_rms(values):
    return lax.rsqrt(jnp.mean(values * values, axis=-1, keepdims=True) + EPSILON)


def norm_back(raw, gain, grad):
    inverse = inverse_rms(raw)
    unit = raw * inverse
    scaled = grad * gain
    back = inverse * (scaled - unit * jnp.mean(scaled * unit, axis=-1, keepdims=True))
    return back, grad * unit


def dot(left, right, contract=(1, 0)):
    dims = (((contract[0],), (contract[1],)), ((), ()))
    return lax.dot_general(left, right, dims, preferred_element_type=FULL)


def by_clip(table, clip):
    out = table[0][None]
    for k in range(1, table.shape[0]):
        out = jnp.where(clip[:, None] == k, table[k][None], out)
    return out


def clip_sums(values, clip, clips):
    return jnp.stack(
        [jnp.sum(jnp.where(clip[:, None] == k, values, 0.0), axis=0) for k in range(clips)]
    )


def xor_order(blocks, index):
    blocks = list(blocks)
    bit = 1
    while bit < len(blocks):
        on = (index & bit) != 0
        blocks = [jnp.where(on, blocks[j ^ bit], blocks[j]) for j in range(len(blocks))]
        bit *= 2
    return blocks


def pick(stack, index, axis=0):
    return lax.dynamic_index_in_dim(stack, index, axis, keepdims=False)


def make_body(seq_size):
    inner = seq_size // GROUPS

    def hop_outer(x, t):
        pairs = [(i, ((i // inner) ^ t) * inner + i % inner) for i in range(seq_size)]
        return lax.ppermute(x, "seq", pairs)

    def hop_inner(x, t):
        pairs = [(i, (i // inner) * inner + ((i % inner) ^ t)) for i in range(seq_size)]
        return lax.ppermute(x, "seq", pairs)

    def hop_core(x):
        return lax.ppermute(x, "head", [(0, 1), (1, 0)])

    def gather_outer(x):
        return [x] + [hop_outer(x, t) for t in range(1, GROUPS)]

    def gather_inner(x):
        return [x] + [hop_inner(x, t) for t in range(1, inner)]

    def gather_tokens(x):
        near = jnp.concatenate(gather_outer(x))
        return jnp.concatenate([near, hop_core(near)])

    def scatter_tokens(partial):
        half = partial.shape[0] // 2
        near = partial[:half] + hop_core(partial[half:].astype(LOW)).astype(FULL)
        parts = near.reshape(GROUPS, half // GROUPS, near.shape[-1])
        total = parts[0]
        for t in range(1, GROUPS):
            total = total + hop_outer(parts[t].astype(LOW), t).astype(FULL)
        return total

    def scatter_inner(parts):
        total = parts[0]
        for t in range(1, inner):
            total = total + hop_inner(parts[t].astype(LOW), t).astype(FULL)
        return total

    def body(
        latents,
        caption,
        conditioning,
        clip_frames,
        valid_patches,
        query_proj,
        key_proj,
        value_proj,
        output_proj,
        caption_key,
        caption_value,
        gate_proj,
        up_proj,
        down_proj,
        modulation,
        query_gain,
        key_gain,
        caption_gain,
        attn_gain,
        ffn_gain,
        cross_gate,
        cotangent,
    ):
        rows, width = latents.shape
        half = rows // 2
        hd = query_gain.shape[0]
        heads = cross_gate.shape[0] // GROUPS
        inner_width = heads * hd
        clips = conditioning.shape[0]
        scale = 1.0 / math.sqrt(hd)
        seq = lax.axis_index("seq")
        core = lax.axis_index("head")
        o, p = seq // inner, seq % inner
        group_rows = GROUPS * rows

        def token_ids(plane):
            c_at = core ^ jnp.arange(2)[:, None, None]
            o_at = o ^ jnp.arange(GROUPS)[None, :, None]
            at = jnp.arange(half)[None, None, :]
            return ((o_at * inner + plane) * rows + c_at * half + at).reshape(-1).astype(jnp.int32)

        ids = token_ids(p)
        key_ids = jnp.concatenate([token_ids(p ^ t) for t in range(inner)])
        clip, position, _ = token_layout(clip_frames, valid_patches, ids)
        _, _, tag = token_layout(clip_frames, valid_patches, key_ids)
        own_clip = clip[:half]

        own = lax.dynamic_slice_in_dim(latents, core * half, half, 0)
        own_cot = lax.dynamic_slice_in_dim(cotangent, core * half, half, 0)
        group_latents = gather_tokens(own).astype(FULL)

        silu_cond = jax.nn.silu(conditioning.astype(FULL)).astype(LOW)
        cond_rows = modulation.shape[0]
        silu_own = lax.dynamic_slice_in_dim(silu_cond, seq * cond_rows, cond_rows, 1)
        shifts = dot(silu_own, modulation)
        shifts = sum(gather_outer(shifts))
        shifts = sum(gather_inner(shifts))
        scale_attn, gate_attn, scale_ffn, gate_ffn = [
            shifts[:, k * width : (k + 1) * width] for k in range(4)
        ]
        first_table = attn_gain * (1.0 + scale_attn)
        second_table = ffn_gain * (1.0 + scale_ffn)
        attn_tanh_table = jnp.tanh(gate_attn)
        ffn_tanh_table = jnp.tanh(gate_ffn)

        def collect(parts):
            piece = parts[0].shape[0]
            send = jnp.concatenate([w.reshape(piece, GROUPS, -1) for w in parts], axis=-1)
            got = [pick(send, o, 1)]
            got += [hop_outer(pick(send, o ^ t, 1), t) for t in range(1, GROUPS)]
            mine = jnp.stack(xor_order(got, o))
            blocks = jnp.stack(xor_order(gather_inner(mine), p), axis=1)
            return blocks.reshape(seq_size * piece, -1)

        attn_weights = collect((query_proj, key_proj, value_proj, output_proj.T))
        ffn_weights = collect((gate_proj, up_proj, down_proj.T))
        qkv = attn_weights[:, : 3 * inner_width]
        out_t = attn_weights[:, 3 * inner_width :]
        hidden_width = ffn_weights.shape[1] // 3
        gate_up = ffn_weights[:, : 2 * hidden_width]
        down_t = ffn_weights[:, 2 * hidden_width :]

        text_own = caption.shape[0]
        cap_cols = caption.shape[1] // seq_size
        cap_split = caption.reshape(text_own, GROUPS, inner, cap_cols)
        cap = [pick(cap_split, o, 1)]
        cap += [hop_outer(pick(cap_split, o ^ t, 1), t) for t in range(1, GROUPS)]
        cap = jnp.concatenate(cap)
        got = [pick(cap, p, 1)]
        got += [hop_inner(pick(cap, p ^ t, 1), t) for t in range(1, inner)]
        cap_mine = jnp.concatenate(got)
        text_group = GROUPS * text_own
        cap_part = jnp.concatenate([dot(cap_mine, caption_key), dot(cap_mine, caption_value)], 1)
        cap_sum = scatter_inner(
            [cap_part[t * text_group : (t + 1) * text_group] for t in range(inner)]
        )
        cap_sum = cap_sum.reshape(GROUPS, text_own, 2, GROUPS, inner_width)
        cap_raw = pick(cap_sum, o, 3)
        for t in range(1, GROUPS):
            sent = jnp.stack([pick(cap_sum[j ^ t], o ^ t, 2) for j in range(GROUPS)])
            cap_raw = cap_raw + hop_outer(sent.astype(LOW), t).astype(FULL)
        cap_raw = cap_raw.reshape(text_group, 2, inner_width)
        cap_key_raw = cap_raw[:, 0].reshape(text_group, heads, hd)
        cap_keys_own = (cap_key_raw * inverse_rms(cap_key_raw) * caption_gain).astype(LOW)
        cap_both = jnp.concatenate(
            [cap_keys_own.reshape(text_group, inner_width), cap_raw[:, 1].astype(LOW)], axis=1
        )
        cap_both = jnp.concatenate(gather_inner(cap_both))
        text_rows = cap_both.shape[0]
        cap_keys = cap_both[:, :inner_width].reshape(text_rows, heads, hd)
        cap_values = cap_both[:, inner_width:].reshape(text_rows, heads, hd)
        p_at = p ^ jnp.arange(inner)[:, None, None]
        o_at = o ^ jnp.arange(GROUPS)[None, :, None]
        text_ids = (o_at * inner + p_at) * text_own + jnp.arange(text_own)[None, None, :]
        text_clip = (text_ids // TEXT).reshape(-1)

        first_mult = by_clip(first_table, clip)
        normed = (group_latents * inverse_rms(group_latents) * first_mult).astype(LOW)
        raw = dot(normed, qkv)
        query_raw = raw[:, :inner_width].reshape(group_rows, heads, hd)
        key_raw = raw[:, inner_width : 2 * inner_width].reshape(group_rows, heads, hd)
        values_own = raw[:, 2 * inner_width :].astype(LOW)
        rates = 10000.0 ** (-(jnp.arange(hd // 2, dtype=FULL) * 2.0 / hd))
        angle = position.astype(FULL)[:, None] * rates[None, :]
        cosine, sine = jnp.cos(angle)[:, None, :], jnp.sin(angle)[:, None, :]
        queries = rotate(query_raw * inverse_rms(query_raw) * query_gain, cosine, sine).astype(LOW)
        keys_own = rotate(key_raw * inverse_rms(key_raw) * key_gain, cosine, sine).astype(LOW)
        both = jnp.concatenate([keys_own.reshape(group_rows, inner_width), values_own], axis=1)
        both = jnp.concatenate(gather_inner(both))
        keys = both[:, :inner_width].reshape(-1, heads, hd)
        values = both[:, inner_width:].reshape(-1, heads, hd)

        gate_here = pick(cross_gate.reshape(GROUPS, heads), o)
        cross_tanh = jnp.tanh(gate_here)

        def weights_of(key_heads, allowed):
            scores = jnp.einsum("qhd,khd->hqk", queries, key_heads, preferred_element_type=FULL)
            return jnp.where(allowed[None], jnp.exp(scores * scale), 0.0)

        def average(weights, value_heads):
            total = jnp.sum(weights, axis=-1)
            out = jnp.einsum(
                "hqk,khd->qhd", weights.astype(LOW), value_heads, preferred_element_type=FULL
            )
            return out / total.T[:, :, None], total

        self_weights = weights_of(keys, clip[:, None] == tag[None, :])
        cross_weights = weights_of(cap_keys, clip[:, None] == text_clip[None, :])
        self_out, self_total = average(self_weights, values)
        cross_out, cross_total = average(cross_weights, cap_values)
        gates = cross_tanh[None, :, None]
        mixed = (self_out + gates * cross_out).astype(LOW).reshape(group_rows, inner_width)
        attended = scatter_tokens(dot(mixed, out_t, (1, 1)))

        inputs = own.astype(FULL)
        upstream = own_cot.astype(FULL)
        attn_tanh = by_clip(attn_tanh_table, own_clip)
        hidden = inputs + attn_tanh * attended
        second_mult = by_clip(second_table, own_clip)
        ffn_own = (hidden * inverse_rms(hidden) * second_mult).astype(LOW)
        ffn_tanh = by_clip(ffn_tanh_table, own_clip)
        d_ffn = gather_tokens((ffn_tanh * upstream).astype(LOW))
        ffn_input = gather_tokens(ffn_own)
        gate_up_val = dot(ffn_input, gate_up)
        gate_val, up_val = gate_up_val[:, :hidden_width], gate_up_val[:, hidden_width:]
        sigma = jax.nn.sigmoid(gate_val)
        activation = (gate_val * sigma * up_val).astype(LOW)
        d_act = dot(d_ffn, down_t)
        d_gate = (d_act * up_val * sigma * (1.0 + gate_val * (1.0 - sigma))).astype(LOW)
        d_up = (d_act * gate_val * sigma).astype(LOW)
        d_gate_up = jnp.concatenate([d_gate, d_up], axis=1)
        d_ffn_input = scatter_tokens(dot(d_gate_up, gate_up, (1, 1)))
        ffn_out = scatter_tokens(dot(activation, down_t, (1, 1)))
        output = (hidden + ffn_tanh * ffn_out).astype(LOW)

        def reduce_matrix(partial, out_widths):
            columns = partial.shape[1]
            parts = partial.reshape(GROUPS, inner, -1, columns)
            total = scatter_inner([pick(parts, p ^ t if t else p, 1) for t in range(inner)])
            got = [pick(total, o)]
            got += [
                hop_outer(pick(total, o ^ t).astype(LOW), t).astype(FULL) for t in range(1, GROUPS)
            ]
            stacked = jnp.stack(xor_order(got, o), axis=1)
            outs, at = [], 0
            for w in out_widths:
                outs.append(stacked[:, :, at : at + w].reshape(stacked.shape[0], -1))
                at += w
            return outs

        ffn_grads = jnp.concatenate(
            [dot(ffn_input, d_gate_up, (0, 0)), dot(d_ffn, activation, (0, 0))], axis=1
        )
        grad_gate, grad_up, grad_down_t = reduce_matrix(ffn_grads, (hidden_width,) * 3)

        second_back, second_terms = norm_back(hidden, second_mult, d_ffn_input)
        ffn_gain_part = jnp.sum(second_terms * (1.0 + by_clip(scale_ffn, own_clip)), axis=0)
        d_hidden = upstream + second_back
        d_attended_own = (attn_tanh * d_hidden).astype(LOW)
        d_attended = gather_tokens(d_attended_own)

        d_mixed = dot(d_attended, out_t).astype(LOW).reshape(group_rows, heads, hd)
        grad_out_t = dot(d_attended, mixed, (0, 0))
        d_mixed_f = d_mixed.astype(FULL)
        cross_gate_part = jnp.sum(d_mixed_f * cross_out, axis=(0, 2)) * (1 - cross_tanh**2)
        d_cross = (gates * d_mixed_f).astype(LOW)

        def attend_back(weights, total, grad, out, key_heads, value_heads):
            prob = weights / total[:, :, None]
            delta = jnp.sum(grad.astype(FULL) * out, axis=-1).T
            d_prob = jnp.einsum("qhd,khd->hqk", grad, value_heads, preferred_element_type=FULL)
            ds = (prob * (d_prob - delta[:, :, None])).astype(LOW)
            dq = jnp.einsum("hqk,khd->qhd", ds, key_heads, preferred_element_type=FULL) * scale
            dk = jnp.einsum("hqk,qhd->khd", ds, queries, preferred_element_type=FULL) * scale
            dv = jnp.einsum("hqk,qhd->khd", prob.astype(LOW), grad, preferred_element_type=FULL)
            flat = lambda x: x.reshape(x.shape[0], inner_width)
            return dq, jnp.concatenate([flat(dk), flat(dv)], axis=1)

        dq_cross, cap_back = attend_back(
            cross_weights, cross_total, d_cross, cross_out, cap_keys, cap_values
        )
        dq_self, kv_back = attend_back(self_weights, self_total, d_mixed, self_out, keys, values)
        kv_back = scatter_inner(
            [kv_back[t * group_rows : (t + 1) * group_rows] for t in range(inner)]
        )
        cap_back = scatter_inner(
            [cap_back[t * text_group : (t + 1) * text_group] for t in range(inner)]
        )

        d_cap_raw, cap_terms = norm_back(
            cap_key_raw, caption_gain, cap_back[:, :inner_width].reshape(text_group, heads, hd)
        )
        d_cap = jnp.concatenate(
            [d_cap_raw.reshape(text_group, inner_width), cap_back[:, inner_width:]], axis=1
        ).astype(LOW)
        got = [d_cap]
        for t in range(1, GROUPS):
            other = hop_outer(d_cap, t).reshape(GROUPS, text_own, -1)
            got.append(jnp.concatenate([other[j ^ t] for j in range(GROUPS)]))
        d_cap = jnp.stack(xor_order(got, o), axis=1)
        d_cap = jnp.concatenate(
            [d_cap[:, :, :inner_width].reshape(text_group, -1), d_cap[:, :, inner_width:].reshape(text_group, -1)],
            axis=1,
        )
        d_cap = jnp.concatenate(gather_inner(d_cap))
        grad_cap = dot(cap_mine, d_cap, (0, 0))
        cap_width = caption_key.shape[1]

        d_query_raw, query_terms = norm_back(
            query_raw, query_gain, rotate(dq_self + dq_cross, cosine, -sine)
        )
        d_key = kv_back[:, :inner_width].reshape(group_rows, heads, hd)
        d_key_raw, key_terms = norm_back(key_raw, key_gain, rotate(d_key, cosine, -sine))
        d_qkv = jnp.concatenate(
            [
                d_query_raw.reshape(group_rows, inner_width),
                d_key_raw.reshape(group_rows, inner_width),
                kv_back[:, inner_width:],
            ],
            axis=1,
        ).astype(LOW)
        d_normed = scatter_tokens(dot(d_qkv, qkv, (1, 1)))
        attn_grads = jnp.concatenate([dot(normed, d_qkv, (0, 0)), grad_out_t], axis=1)
        grad_query, grad_key, grad_value, grad_output_t = reduce_matrix(
            attn_grads, (inner_width,) * 4
        )

        own_mult = by_clip(first_table, own_clip)
        first_back, first_terms = norm_back(inputs, own_mult, d_normed)
        grad_latents = (d_hidden + first_back).astype(LOW)
        attn_gain_part = jnp.sum(first_terms * (1.0 + by_clip(scale_attn, own_clip)), axis=0)

        token_grads = jnp.concatenate(
            [
                first_terms * attn_gain,
                d_hidden * attended * (1.0 - attn_tanh * attn_tanh),
                second_terms * ffn_gain,
                upstream * ffn_out * (1.0 - ffn_tanh * ffn_tanh),
            ],
            axis=1,
        )
        gate_slots = jnp.arange(2 * GROUPS) == core * GROUPS + o
        small = [
            clip_sums(token_grads, own_clip, clips).reshape(-1),
            attn_gain_part,
            ffn_gain_part,
            jnp.sum(query_terms, axis=(0, 1)),
            jnp.sum(key_terms, axis=(0, 1)),
            jnp.sum(cap_terms, axis=(0, 1)),
            jnp.where(gate_slots[:, None], cross_gate_part[None, :], 0.0).reshape(-1),
        ]
        sizes = [x.shape[0] for x in small]
        small = jnp.concatenate(small)
        small = small + hop_core(small)
        small = sum(xor_order(gather_outer(small), o))
        small = sum(xor_order(gather_inner(small), p))
        pieces, at = [], 0
        for n in sizes:
            pieces.append(small[at : at + n])
            at += n
        shift_grad, g_attn, g_ffn, g_query, g_key, g_cap, g_cross = pieces
        shift_grad = shift_grad.reshape(clips, 4 * width)
        g_cross = pick(g_cross.reshape(2, -1), core)
        silu_f = silu_own.astype(FULL)
        grad_modulation = sum(silu_f[k][:, None] * shift_grad[k][None, :] for k in range(clips))

        def whole_rows(x):
            both = jnp.stack([x, hop_core(x)])
            return jnp.concatenate([pick(both, core), pick(both, 1 - core)])

        return (
            whole_rows(output),
            whole_rows(grad_latents),
            grad_query,
            grad_key,
            grad_value,
            grad_output_t.T,
            grad_cap[:, :cap_width],
            grad_cap[:, cap_width:],
            grad_gate,
            grad_up,
            grad_down_t.T,
            grad_modulation,
            g_query,
            g_key,
            g_cap,
            g_attn,
            g_ffn,
            g_cross,
        )

    return body


def solution(mesh):
    rows, cols, turned = P("seq", None), P("seq", "head"), P("head", "seq")
    one = P()
    placed = (rows, rows, one, one, one, cols, cols, cols, turned, cols, cols, cols, cols, turned)
    placed += (rows, one, one, one, one, one, P("head"), rows)
    given = (rows, rows, cols, cols, cols, turned, cols, cols, cols, cols, turned, rows)
    given += (one, one, one, one, one, P("head"))
    return jax.shard_map(
        make_body(mesh.shape["seq"]), mesh=mesh, in_specs=placed, out_specs=given, check_vma=False
    )
```

time: 3070 us -> 593 us (0.19)
  waiting for transfers between devices: 2370 us -> 245 us
  blocking collectives: 326 us -> 0 us
  matrix products: 199 us -> 52.7 us
  starting transfers between devices: 1.55 us -> 132 us
    reduce_scatter x10 -> x0, waiting for transfers between devices: 1530 us -> none  [the longest x1 211 us: body(): lax.psum_scatter(grad_down, 'seq', scatter_dimension=1, tiled=True)]
    all_gather x14 -> x0, waiting for transfers between devices: 817 us -> none  [the longest x1 150 us: body(): lax.all_gather(modulation, 'seq', axis=0, tiled=True)]
    ppermute x0 -> x101, waiting for transfers between devices: none -> 245 us  [the longest x51 155 us: hop_outer(): return lax.ppermute(x, 'seq', pairs)]
    all_gather x6 -> x0, blocking collectives: 245 us -> none  [the longest x1 46.9 us: body(): lax.all_gather(caption_keys_own, 'seq', axis=0, tiled=True)]
    dot_general x68 -> x28, matrix products: 199 us -> 52.7 us  [the longest x16 26.6 us: dot(): return lax.dot_general(left, right, dims, preferred_element_type=FULL)]
    ppermute x0 -> x101, starting transfers between devices: none -> 132 us  [the longest x51 77.8 us: hop_outer(): return lax.ppermute(x, 'seq', pairs)]
    psum x2 -> x0, blocking collectives: 81.8 us -> none  [the longest x1 79.3 us: body(): lax.psum((shift_part, attn_gain_part, ffn_gain_part, cross_gate_part, gai...]
    dynamic_slice x32 -> x6, local copies, waits for them, and re-layouts: 48.9 us -> 1.21 us  [pick(): return lax.dynamic_index_in_dim(stack, index, axis, keepdims=False)]
  transfers between devices with their start and end apart: 27 -> 101, of which waited for: 23 -> 39; matrix products, arithmetic and copies ran while one was open for 10% -> 26% of each run, Pallas kernels for 0% -> 0%
where the time goes in v1:
time: 593 us; the launch traced here: 583 us
  waiting for transfers between devices  245 us (41%)
  starting transfers between devices  132 us (22%)
  local copies, waits for them, and re-layouts  84.9 us (14%)
  other arithmetic  64.1 us (11%)
  matrix products  52.7 us (9%)
    ppermute x51, waiting for transfers between devices, hop_outer(): return lax.ppermute(x, 'seq', pairs)  155 us
    ppermute x39, waiting for transfers between devices, hop_inner(): return lax.ppermute(x, 'seq', pairs)  87.8 us
    ppermute x51, starting transfers between devices, hop_outer(): return lax.ppermute(x, 'seq', pairs)  77.8 us
    ppermute x39, starting transfers between devices, hop_inner(): return lax.ppermute(x, 'seq', pairs)  52.9 us
    dot_general x16, matrix products, dot(): return lax.dot_general(left, right, dims, preferred_element_type=FULL)  26.6 us
    unnamed x373, local copies, waits for them, and re-layouts  12.4 us
  transfers between devices with their start and end apart: 101, of which 39 were waited for; matrix products, arithmetic and copies ran while one was open for 26% of the time, Pallas kernels for 0%

profile of v1, /device:TPU:0, one launch (start us, length us, event | category | flops | bytes accessed | tf_op | source)
XLA Modules:
  0.0 583.2 jit_solution(4738424397871586452)
XLA Ops:
  61.9 12.1 %collective-permute-done.11 = bf16[96,768]{1,0:T(8,128)(2,1)S(1)} collective-permute-done((bf16[96,768]{1,0:T(8,128)(2,1)}, bf16[96,768]{1,0:T(8,128)(2,1)S(1)}, u32[]{:S(2)}, u32[]{:S(2)}) %collective-permute-start.11) | collective-permute-done | bytes 147488 | tf_op jit(solution)/shard_map/ppermute | solution.py:85
  84.9 4.8 collective-permute-done.26
  97.9 7.3 %collective-permute-done.28 = bf16[4,32,2,192]{3,1,2,0:T(8,128)(2,1)S(1)} collective-permute-done((bf16[4,32,2,192]{3,1,2,0:T(8,128)(2,1)S(1)}, bf16[4,32,2,192]{3,1,2,0:T(8,128)(2,1)S(1)}, u32[]{:S(2)}, u32[]{:S(2)}) %collective-permute-start.28) | collective-permute-done | bytes 98336 | tf_op jit(solution)/shard_map/ppermute | solution.py:85
  114.1 16.0 %collective-permute-done.31 = bf16[128,384]{1,0:T(8,128)(2,1)S(1)} collective-permute-done((bf16[128,384]{1,0:T(8,128)(2,1)S(1)}, bf16[128,384]{1,0:T(8,128)(2,1)S(1)}, u32[]{:S(2)}, u32[]{:S(2)}) %collective-permute-start.31) | collective-permute-done | bytes 98336 | tf_op jit(solution)/shard_map/ppermute | solution.py:89
  156.7 17.7 %collective-permute-done.16 = bf16[512,384]{0,1:T(8,128)(2,1)S(1)} collective-permute-done((bf16[512,384]{0,1:T(8,128)(2,1)S(1)}, bf16[512,384]{0,1:T(8,128)(2,1)S(1)}, u32[]{:S(2)}, u32[]{:S(2)}) %collective-permute-start.16) | collective-permute-done | bytes 393248 | tf_op jit(solution)/shard_map/ppermute | solution.py:89
  174.9 29.7 %collective-permute-done.17 = bf16[512,384]{0,1:T(8,128)(2,1)S(1)} collective-permute-done((bf16[512,384]{0,1:T(8,128)(2,1)S(1)}, bf16[512,384]{0,1:T(8,128)(2,1)S(1)}, u32[]{:S(2)}, u32[]{:S(2)}) %collective-permute-start.17) | collective-permute-done | bytes 393248 | tf_op jit(solution)/shard_map/ppermute | solution.py:89
  229.3 7.3 %collective-permute-done.36 = bf16[64,1536]{1,0:T(8,128)(2,1)S(1)} collective-permute-done((bf16[64,1536]{1,0:T(8,128)(2,1)S(1)}, bf16[64,1536]{1,0:T(8,128)(2,1)S(1)}, u32[]{:S(2)}, u32[]{:S(2)}) %collective-permute-start.36) | collective-permute-done | bytes 196640 | tf_op jit(solution)/shard_map/ppermute | solution.py:85
  252.5 5.9 %collective-permute-done.54 = bf16[64,1536]{1,0:T(8,128)(2,1)S(1)} collective-permute-done((bf16[64,1536]{1,0:T(8,128)(2,1)S(1)}, bf16[64,1536]{1,0:T(8,128)(2,1)S(1)}, u32[]{:S(2)}, u32[]{:S(2)}) %collective-permute-start.54) | collective-permute-done | bytes 196640 | tf_op jit(solution)/shard_map/ppermute | solution.py:85
  259.2 15.8 %collective-permute-done.39 = bf16[64,1536]{1,0:T(8,128)(2,1)S(1)} collective-permute-done((bf16[64,1536]{1,0:T(8,128)(2,1)S(1)}, bf16[64,1536]{1,0:T(8,128)(2,1)S(1)}, u32[]{:S(2)}, u32[]{:S(2)}) %collective-permute-start.39) | collective-permute-done | bytes 196640 | tf_op jit(solution)/shard_map/ppermute | solution.py:85
  282.5 4.5 fusion.79
  291.5 7.2 %pad_maximum_fusion = f32[1536,1536]{0,1:T(8,128)} fusion(f32[1536,512]{0,1:T(8,128)S(1)} %fusion.217, f32[1536,1024]{0,1:T(8,128)} %fusion.79), kind=kLoop, calls=%fused_computation.2 | loop fusion | flops 2359296 | bytes 18874368 | tf_op jit(solution)/shard_map/concatenate | solution.py:310
  298.7 9.8 %copy.248 = f32[1536,1536]{1,0:T(8,128)} copy(f32[1536,1536]{0,1:T(8,128)} %pad_maximum_fusion) | data formatting | bytes 18874368 | tf_op jit(solution)/shard_map/concatenate | solution.py:310
  320.7 4.6 collective-permute-done.58
  325.3 9.3 %collective-permute-done.59 = bf16[64,1536]{1,0:T(8,128)(2,1)S(1)} collective-permute-done((bf16[64,1536]{1,0:T(8,128)(2,1)S(1)}, bf16[64,1536]{1,0:T(8,128)(2,1)S(1)}, u32[]{:S(2)}, u32[]{:S(2)}) %collective-permute-start.59) | collective-permute-done | bytes 196640 | tf_op jit(solution)/shard_map/ppermute | solution.py:85
  339.7 11.8 %collective-permute-done.50 = bf16[64,1536]{1,0:T(8,128)(2,1)S(1)} collective-permute-done((bf16[64,1536]{1,0:T(8,128)(2,1)S(1)}, bf16[64,1536]{1,0:T(8,128)(2,1)S(1)}, u32[]{:S(2)}, u32[]{:S(2)}) %collective-permute-start.50) | collective-permute-done | bytes 196640 | tf_op jit(solution)/shard_map/ppermute | solution.py:85
  367.4 8.2 %collective-permute-done.62 = bf16[64,1536]{1,0:T(8,128)(2,1)S(1)} collective-permute-done((bf16[64,1536]{1,0:T(8,128)(2,1)S(1)}, bf16[64,1536]{1,0:T(8,128)(2,1)S(1)}, u32[]{:S(2)}, u32[]{:S(2)}) %collective-permute-start.62) | collective-permute-done | bytes 196640 | tf_op jit(solution)/shard_map/ppermute | solution.py:85
  382.9 7.0 %collective-permute-done.91 = bf16[96,1536]{1,0:T(8,128)(2,1)S(1)} collective-permute-done((bf16[96,1536]{1,0:T(8,128)(2,1)S(1)}, bf16[96,1536]{1,0:T(8,128)(2,1)S(1)}, u32[]{:S(2)}, u32[]{:S(2)}) %collective-permute-start.91) | collective-permute-done | bytes 294944 | tf_op jit(solution)/shard_map/ppermute | solution.py:85
  389.9 18.4 %collective-permute-done.92 = bf16[96,1536]{1,0:T(8,128)(2,1)S(1)} collective-permute-done((bf16[96,1536]{1,0:T(8,128)(2,1)S(1)}, bf16[96,1536]{1,0:T(8,128)(2,1)S(1)}, u32[]{:S(2)}, u32[]{:S(2)}) %collective-permute-start.92) | collective-permute-done | bytes 294944 | tf_op jit(solution)/shard_map/ppermute | solution.py:85
  424.8 4.6 multiply_convert_fusion
  477.3 8.5 %collective-permute-start.85 = (bf16[128,1536]{0,1:T(8,128)(2,1)}, bf16[128,1536]{0,1:T(8,128)(2,1)}, u32[]{:S(2)}, u32[]{:S(2)}) collective-permute-start(bf16[128,1536]{0,1:T(8,128)(2,1)} %pad_maximum_fusion.29), channel_id=1, source_target_pairs={{0,2},{2,0},{4,6},{6,4},{8,10},{10,8},{12,14},{14,12},{16,18},{18,... | collective-permute-start | bytes 1179656 | tf_op jit(solution)/shard_map/ppermute | solution.py:89
  495.5 6.3 %copy.232 = f32[1536,768]{1,0:T(8,128)} copy(f32[1536,768]{0,1:T(8,128)} %pad_maximum_fusion.2) | data formatting | bytes 9437184 | tf_op jit(solution)/shard_map/concatenate | solution.py:382
  518.6 5.9 %collective-permute-done.74 = bf16[4,96,768]{2,1,0:T(8,128)(2,1)} collective-permute-done((bf16[4,96,768]{2,1,0:T(8,128)(2,1)}, bf16[4,96,768]{2,1,0:T(8,128)(2,1)}, u32[]{:S(2)}, u32[]{:S(2)}) %collective-permute-start.74) | collective-permute-done | bytes 589856 | tf_op jit(solution)/shard_map/ppermute | solution.py:89
  535.2 7.7 %collective-permute-done.77 = bf16[96,768]{1,0:T(8,128)(2,1)S(1)} collective-permute-done((bf16[96,768]{1,0:T(8,128)(2,1)S(1)}, bf16[96,768]{1,0:T(8,128)(2,1)S(1)}, u32[]{:S(2)}, u32[]{:S(2)}) %collective-permute-start.77) | collective-permute-done | bytes 147488 | tf_op jit(solution)/shard_map/ppermute | solution.py:85
  545.0 6.1 %collective-permute-done.70 = bf16[64,1536]{1,0:T(8,128)(2,1)S(1)} collective-permute-done((bf16[64,1536]{1,0:T(8,128)(2,1)S(1)}, bf16[64,1536]{1,0:T(8,128)(2,1)S(1)}, u32[]{:S(2)}, u32[]{:S(2)}) %collective-permute-start.70) | collective-permute-done | bytes 196640 | tf_op jit(solution)/shard_map/ppermute | solution.py:85
  (835 shorter events, 342.3 us)
Async XLA Ops:
  3.0 29.6 %collective-permute-start = (f32[2,6144]{1,0:T(2,128)}, f32[2,6144]{1,0:T(2,128)}, u32[]{:S(2)}, u32[]{:S(2)}) collective-permute-start(f32[2,6144]{1,0:T(2,128)} %fusion.215), channel_id=1, source_target_pairs={{0,8},{2,10},{4,12},{6,14},{8,0},{10,2},{12,4},{14,6},{16,24},{18,... | collective-permute-start | bytes 147464 | tf_op jit(solution)/shard_map/ppermute | solution.py:85
  10.2 66.9 %collective-permute-start.6 = (bf16[64,1536]{1,0:T(8,128)(2,1)S(1)}, bf16[64,1536]{1,0:T(8,128)(2,1)S(1)}, u32[]{:S(2)}, u32[]{:S(2)}) collective-permute-start(bf16[64,1536]{1,0:T(8,128)(2,1)S(1)} %get-tuple-element.50), channel_id=1, source_target_pairs={{0,8},{2,10},{4,12},{6,14},{8,0},{10,2},{12,4},{14,6},{16,24},{18,... | collective-permute-start | bytes 589832 | tf_op jit(solution)/shard_map/ppermute | solution.py:85
  11.1 66.6 %collective-permute-start.7 = (bf16[64,1536]{1,0:T(8,128)(2,1)S(1)}, bf16[64,1536]{1,0:T(8,128)(2,1)S(1)}, u32[]{:S(2)}, u32[]{:S(2)}) collective-permute-start(bf16[64,1536]{1,0:T(8,128)(2,1)S(1)} %get-tuple-element.50), channel_id=1, source_target_pairs={{0,16},{2,18},{4,20},{6,22},{8,24},{10,26},{12,28},{14,30},{16,0},... | collective-permute-start | bytes 589832 | tf_op jit(solution)/shard_map/ppermute | solution.py:85
  74.1 34.3 %collective-permute-start.42 = (bf16[96,1536]{1,0:T(8,128)(2,1)}, bf16[96,1536]{1,0:T(8,128)(2,1)}, u32[]{:S(2)}, u32[]{:S(2)}) collective-permute-start(bf16[96,1536]{1,0:T(8,128)(2,1)} %get-tuple-element.127), channel_id=1, source_target_pairs={{0,24},{2,26},{4,28},{6,30},{8,16},{10,18},{12,20},{14,22},{16,8},... | collective-permute-start | bytes 884744 | tf_op jit(solution)/shard_map/ppermute | solution.py:85
  76.1 33.9 %collective-permute-start.43 = (bf16[96,1536]{1,0:T(8,128)(2,1)}, bf16[96,1536]{1,0:T(8,128)(2,1)}, u32[]{:S(2)}, u32[]{:S(2)}) collective-permute-start(bf16[96,1536]{1,0:T(8,128)(2,1)} %get-tuple-element.126), channel_id=1, source_target_pairs={{0,16},{2,18},{4,20},{6,22},{8,24},{10,26},{12,28},{14,30},{16,0},... | collective-permute-start | bytes 884744 | tf_op jit(solution)/shard_map/ppermute | solution.py:85
  105.2 36.8 %collective-permute-start.13 = (bf16[4,96,768]{2,1,0:T(8,128)(2,1)}, bf16[4,96,768]{2,1,0:T(8,128)(2,1)S(1)}, u32[]{:S(2)}, u32[]{:S(2)}) collective-permute-start(bf16[4,96,768]{2,1,0:T(8,128)(2,1)} %pad_maximum_fusion.20), channel_id=1, source_target_pairs={{0,6},{2,4},{4,2},{6,0},{8,14},{10,12},{12,10},{14,8},{16,22},{18,... | collective-permute-start | bytes 1769480 | tf_op jit(solution)/shard_map/ppermute | solution.py:89
  106.0 36.6 %collective-permute-start.14 = (bf16[4,96,768]{2,1,0:T(8,128)(2,1)}, bf16[4,96,768]{2,1,0:T(8,128)(2,1)S(1)}, u32[]{:S(2)}, u32[]{:S(2)}) collective-permute-start(bf16[4,96,768]{2,1,0:T(8,128)(2,1)} %pad_maximum_fusion.20), channel_id=1, source_target_pairs={{0,4},{2,6},{4,0},{6,2},{8,12},{10,14},{12,8},{14,10},{16,20},{18,... | collective-permute-start | bytes 1769480 | tf_op jit(solution)/shard_map/ppermute | solution.py:89
  108.4 34.2 %collective-permute-start.15 = (bf16[4,96,768]{2,1,0:T(8,128)(2,1)}, bf16[4,96,768]{2,1,0:T(8,128)(2,1)S(1)}, u32[]{:S(2)}, u32[]{:S(2)}) collective-permute-start(bf16[4,96,768]{2,1,0:T(8,128)(2,1)} %pad_maximum_fusion.20), channel_id=1, source_target_pairs={{0,2},{2,0},{4,6},{6,4},{8,10},{10,8},{12,14},{14,12},{16,18},{18,... | collective-permute-start | bytes 1769480 | tf_op jit(solution)/shard_map/ppermute | solution.py:89
  135.6 81.0 %collective-permute-start.45 = (bf16[4,96,1536]{2,1,0:T(8,128)(2,1)}, bf16[4,96,1536]{2,1,0:T(8,128)(2,1)}, u32[]{:S(2)}, u32[]{:S(2)}) collective-permute-start(bf16[4,96,1536]{2,1,0:T(8,128)(2,1)} %pad_maximum_fusion.9), channel_id=1, source_target_pairs={{0,6},{2,4},{4,2},{6,0},{8,14},{10,12},{12,10},{14,8},{16,22},{18,... | collective-permute-start | bytes 3538952 | tf_op jit(solution)/shard_map/ppermute | solution.py:89
  142.0 74.6 %collective-permute-start.46 = (bf16[4,96,1536]{2,1,0:T(8,128)(2,1)}, bf16[4,96,1536]{2,1,0:T(8,128)(2,1)S(1)}, u32[]{:S(2)}, u32[]{:S(2)}) collective-permute-start(bf16[4,96,1536]{2,1,0:T(8,128)(2,1)} %pad_maximum_fusion.9), channel_id=1, source_target_pairs={{0,4},{2,6},{4,0},{6,2},{8,12},{10,14},{12,8},{14,10},{16,20},{18,... | collective-permute-start | bytes 3538952 | tf_op jit(solution)/shard_map/ppermute | solution.py:89
  151.8 52.8 %collective-permute-start.17 = (bf16[512,384]{0,1:T(8,128)(2,1)S(1)}, bf16[512,384]{0,1:T(8,128)(2,1)S(1)}, u32[]{:S(2)}, u32[]{:S(2)}) collective-permute-start(bf16[512,384]{0,1:T(8,128)(2,1)S(1)} %pad_maximum_fusion.22), channel_id=1, source_target_pairs={{0,4},{2,6},{4,0},{6,2},{8,12},{10,14},{12,8},{14,10},{16,20},{18,... | collective-permute-start | bytes 1179656 | tf_op jit(solution)/shard_map/ppermute | solution.py:89
  153.6 51.1 %collective-permute-start.18 = (bf16[512,384]{0,1:T(8,128)(2,1)S(1)}, bf16[512,384]{0,1:T(8,128)(2,1)S(1)}, u32[]{:S(2)}, u32[]{:S(2)}) collective-permute-start(bf16[512,384]{0,1:T(8,128)(2,1)S(1)} %pad_maximum_fusion.22), channel_id=1, source_target_pairs={{0,6},{2,4},{4,2},{6,0},{8,14},{10,12},{12,10},{14,8},{16,22},{18,... | collective-permute-start | bytes 1179656 | tf_op jit(solution)/shard_map/ppermute | solution.py:89
  174.4 42.2 %collective-permute-start.47 = (bf16[4,96,1536]{2,1,0:T(8,128)(2,1)}, bf16[4,96,1536]{2,1,0:T(8,128)(2,1)S(1)}, u32[]{:S(2)}, u32[]{:S(2)}) collective-permute-start(bf16[4,96,1536]{2,1,0:T(8,128)(2,1)} %pad_maximum_fusion.9), channel_id=1, source_target_pairs={{0,2},{2,0},{4,6},{6,4},{8,10},{10,8},{12,14},{14,12},{16,18},{18,... | collective-permute-start | bytes 3538952 | tf_op jit(solution)/shard_map/ppermute | solution.py:89
  245.3 29.6 %collective-permute-start.39 = (bf16[64,1536]{1,0:T(8,128)(2,1)S(1)}, bf16[64,1536]{1,0:T(8,128)(2,1)S(1)}, u32[]{:S(2)}, u32[]{:S(2)}) collective-permute-start(bf16[64,1536]{1,0:T(8,128)(2,1)S(1)} %get-tuple-element.237), channel_id=1, source_target_pairs={{0,16},{2,18},{4,20},{6,22},{8,24},{10,26},{12,28},{14,30},{16,0},... | collective-permute-start | bytes 589832 | tf_op jit(solution)/shard_map/ppermute | solution.py:85
  312.3 63.4 %collective-permute-start.88 = (bf16[4,96,1536]{2,1,0:T(8,128)(2,1)S(1)}, bf16[4,96,1536]{2,1,0:T(8,128)(2,1)S(1)}, u32[]{:S(2)}, u32[]{:S(2)}) collective-permute-start(bf16[4,96,1536]{2,1,0:T(8,128)(2,1)S(1)} %get-tuple-element.67), channel_id=1, source_target_pairs={{0,2},{2,0},{4,6},{6,4},{8,10},{10,8},{12,14},{14,12},{16,18},{18,... | collective-permute-start | bytes 3538952 | tf_op jit(solution)/shard_map/ppermute | solution.py:89
  314.1 61.7 %collective-permute-start.89 = (bf16[4,96,1536]{2,1,0:T(8,128)(2,1)S(1)}, bf16[4,96,1536]{2,1,0:T(8,128)(2,1)S(1)}, u32[]{:S(2)}, u32[]{:S(2)}) collective-permute-start(bf16[4,96,1536]{2,1,0:T(8,128)(2,1)S(1)} %get-tuple-element.69), channel_id=1, source_target_pairs={{0,4},{2,6},{4,0},{6,2},{8,12},{10,14},{12,8},{14,10},{16,20},{18,... | collective-permute-start | bytes 3538952 | tf_op jit(solution)/shard_map/ppermute | solution.py:89
  338.4 37.3 %collective-permute-start.90 = (bf16[4,96,1536]{2,1,0:T(8,128)(2,1)S(1)}, bf16[4,96,1536]{2,1,0:T(8,128)(2,1)S(1)}, u32[]{:S(2)}, u32[]{:S(2)}) collective-permute-start(bf16[4,96,1536]{2,1,0:T(8,128)(2,1)S(1)} %get-tuple-element.68), channel_id=1, source_target_pairs={{0,6},{2,4},{4,2},{6,0},{8,14},{10,12},{12,10},{14,8},{16,22},{18,... | collective-permute-start | bytes 3538952 | tf_op jit(solution)/shard_map/ppermute | solution.py:89
  375.6 36.3 %collective-permute-start.64 = (bf16[256,1536]{1,0:T(8,128)(2,1)S(1)}, bf16[256,1536]{1,0:T(8,128)(2,1)S(1)}, u32[]{:S(2)}, u32[]{:S(2)}) collective-permute-start(bf16[256,1536]{1,0:T(8,128)(2,1)S(1)} %pad_maximum_fusion.16), channel_id=1, source_target_pairs={{0,1},{1,0},{2,3},{3,2},{4,5},{5,4},{6,7},{7,6},{8,9},{9,8},{10,11... | collective-permute-start | bytes 2359304 | tf_op jit(solution)/shard_map/ppermute | solution.py:92
  434.8 52.8 %collective-permute-start.65 = (bf16[512,384]{0,1:T(8,128)(2,1)}, bf16[512,384]{0,1:T(8,128)(2,1)}, u32[]{:S(2)}, u32[]{:S(2)}) collective-permute-start(bf16[512,384]{0,1:T(8,128)(2,1)} %get-tuple-element.104), channel_id=1, source_target_pairs={{0,2},{2,0},{4,6},{6,4},{8,10},{10,8},{12,14},{14,12},{16,18},{18,... | collective-permute-start | bytes 1179656 | tf_op jit(solution)/shard_map/ppermute | solution.py:89
  435.4 52.3 %collective-permute-start.66 = (bf16[512,384]{0,1:T(8,128)(2,1)}, bf16[512,384]{0,1:T(8,128)(2,1)}, u32[]{:S(2)}, u32[]{:S(2)}) collective-permute-start(bf16[512,384]{0,1:T(8,128)(2,1)} %get-tuple-element.106), channel_id=1, source_target_pairs={{0,4},{2,6},{4,0},{6,2},{8,12},{10,14},{12,8},{14,10},{16,20},{18,... | collective-permute-start | bytes 1179656 | tf_op jit(solution)/shard_map/ppermute | solution.py:89
  449.1 38.6 %collective-permute-start.67 = (bf16[512,384]{0,1:T(8,128)(2,1)}, bf16[512,384]{0,1:T(8,128)(2,1)}, u32[]{:S(2)}, u32[]{:S(2)}) collective-permute-start(bf16[512,384]{0,1:T(8,128)(2,1)} %get-tuple-element.105), channel_id=1, source_target_pairs={{0,6},{2,4},{4,2},{6,0},{8,14},{10,12},{12,10},{14,8},{16,22},{18,... | collective-permute-start | bytes 1179656 | tf_op jit(solution)/shard_map/ppermute | solution.py:89
  477.3 34.6 %collective-permute-start.85 = (bf16[128,1536]{0,1:T(8,128)(2,1)}, bf16[128,1536]{0,1:T(8,128)(2,1)}, u32[]{:S(2)}, u32[]{:S(2)}) collective-permute-start(bf16[128,1536]{0,1:T(8,128)(2,1)} %pad_maximum_fusion.29), channel_id=1, source_target_pairs={{0,2},{2,0},{4,6},{6,4},{8,10},{10,8},{12,14},{14,12},{16,18},{18,... | collective-permute-start | bytes 1179656 | tf_op jit(solution)/shard_map/ppermute | solution.py:89
  485.9 29.0 %collective-permute-start.86 = (bf16[128,1536]{0,1:T(8,128)(2,1)}, bf16[128,1536]{0,1:T(8,128)(2,1)}, u32[]{:S(2)}, u32[]{:S(2)}) collective-permute-start(bf16[128,1536]{0,1:T(8,128)(2,1)} %pad_maximum_fusion.29), channel_id=1, source_target_pairs={{0,4},{2,6},{4,0},{6,2},{8,12},{10,14},{12,8},{14,10},{16,20},{18,... | collective-permute-start | bytes 1179656 | tf_op jit(solution)/shard_map/ppermute | solution.py:89
  514.9 64.9 %collective-permute-start.52 = (bf16[64,1536]{1,0:T(8,128)(2,1)}, bf16[64,1536]{1,0:T(8,128)(2,1)}, u32[]{:S(2)}, u32[]{:S(2)}) collective-permute-start(bf16[64,1536]{1,0:T(8,128)(2,1)} %get-tuple-element.92), channel_id=1, source_target_pairs={{0,1},{1,0},{2,3},{3,2},{4,5},{5,4},{6,7},{7,6},{8,9},{9,8},{10,11... | collective-permute-start | bytes 589832 | tf_op jit(solution)/shard_map/ppermute | solution.py:92
  (246 other events, 2757.3 us)
